TPU v7x, 32 devices: a whole 2x2x4 slice. The times are simulated.
32 devices in a mesh: ctx: 8 (over y, x, core), mp: 4 (over z).
Axes of the slice: x: 2, y: 2, z: 4, core: 2. Of those that a mesh axis runs over, the one named last changes fastest.
Arguments:
- tokens: bfloat16 [1, 4096, 4096], P(None, 'ctx', 'mp'), may hold values from -40 to 40
- w_branch: bfloat16 [4096, 2048], P(None, 'mp'), may hold values from -0.09375 to 0.09375
- w_input: bfloat16 [4096, 2048], P(None, 'mp'), may hold values from -0.09375 to 0.09375
- conv_kernel: float32 [4, 2048], P(None, 'mp'), may hold values from -3 to 3
- w_rate: bfloat16 [8, 256, 256], P('mp'), may hold values from -0.375 to 0.375
- w_admit: bfloat16 [8, 256, 256], P('mp'), may hold values from -0.375 to 0.375
- lam: float32 [2048], P('mp'), may hold values from 3 to 16
- w_out: bfloat16 [2048, 4096], P('mp'), may hold values from -0.375 to 0.375
- w_query: bfloat16 [4096, 2048], P(None, 'mp'), may hold values from -0.0625 to 0.0625
- w_key: bfloat16 [4096, 256], P(None, 'mp'), may hold values from -4.0625 to 4.0625
- w_value: bfloat16 [4096, 256], P(None, 'mp'), may hold values from -0.09375 to 0.09375
- w_attn_out: bfloat16 [2048, 4096], P('mp'), may hold values from -0.25 to 0.25
Outputs:
- layer_output: bfloat16 [1, 4096, 4096], P(None, 'ctx', 'mp')
All inputs are finite; a program needn't handle non-finite values.
Results may differ from a plain program's by a relative error of at most 0.0065.
Values may be sent and summed in bfloat16 or wider, within the bound.
A program may use at most 128 MiB of HBM per device.

v0:
```python
import jax
import jax.numpy as jnp
from jax import lax
from jax.sharding import PartitionSpec as P

HD = 256
WINDOW = 2048


EPSILON = 1e-06


def from_behind(x, axis, by):
    count = lax.axis_size(axis)
    pairs = [(i, i + by) for i in range(count) if 0 <= i + by < count]
    return lax.ppermute(x, axis, pairs)


def normalize(values):
    wide = values.astype(jnp.float32)
    return wide * lax.rsqrt(jnp.mean(wide * wide, axis=-1, keepdims=True) + EPSILON)


def rotate(values, positions):
    width = values.shape[-1]
    turned = width // 2
    half = turned // 2
    freqs = 10000.0 ** (-jnp.arange(half, dtype=jnp.float32) * 2.0 / turned)
    angles = positions.astype(jnp.float32)[:, None] * freqs[None, :]
    cosine = jnp.cos(angles)[:, None, :]
    sine = jnp.sin(angles)[:, None, :]
    first = values[..., :half]
    second = values[..., half:turned]
    return jnp.concatenate(
        [first * cosine - second * sine, second * cosine + first * sine, values[..., turned:]],
        axis=-1,
    )


def combine_steps(earlier, later):
    return (earlier[0] * later[0], later[0] * earlier[1] + later[1])


def on_device(
    tokens,
    w_branch,
    w_input,
    conv_kernel,
    w_rate,
    w_admit,
    lam,
    w_out,
    w_query,
    w_key,
    w_value,
    w_attn_out,
):
    batch, rows_dev, cols_dev = tokens.shape
    count = batch * rows_dev
    width = w_branch.shape[0]
    full = lax.all_gather(tokens, "mp", axis=2, tiled=True)
    normed = normalize(full).astype(jnp.bfloat16).reshape(count, width)
    branch = jax.nn.gelu(jnp.dot(normed, w_branch, preferred_element_type=jnp.float32))
    inner = jnp.dot(normed, w_input, preferred_element_type=jnp.float32).reshape(
        batch, rows_dev, -1
    )
    taps = conv_kernel.shape[0]
    rim = from_behind(inner[:, rows_dev - taps + 1 :, :], "ctx", 1)
    extended = jnp.concatenate([rim, inner], axis=1)
    convolved = jnp.zeros_like(inner)
    for tap in range(taps):
        convolved = (
            convolved
            + conv_kernel[tap] * extended[:, taps - 1 - tap : taps - 1 - tap + rows_dev, :]
        )
    blocks = w_rate.shape[0]
    block_width = w_rate.shape[1]
    grouped = convolved.astype(jnp.bfloat16).reshape(batch, rows_dev, blocks, block_width)
    rate_gate = jax.nn.sigmoid(
        jnp.einsum("bsnc,ncd->bsnd", grouped, w_rate, preferred_element_type=jnp.float32)
    ).reshape(batch, rows_dev, -1)
    admit_gate = jax.nn.sigmoid(
        jnp.einsum("bsnc,ncd->bsnd", grouped, w_admit, preferred_element_type=jnp.float32)
    ).reshape(batch, rows_dev, -1)
    log_decay = -8.0 * rate_gate * jax.nn.softplus(-lam)
    decay = jnp.exp(log_decay)
    scaled = admit_gate * convolved * jnp.sqrt(-jnp.expm1(2.0 * log_decay))
    cumulative, local_state = lax.associative_scan(combine_steps, (decay, scaled), axis=1)
    through = cumulative[:, -1, :]
    final = local_state[:, -1, :]

    def relay_turn(step, incoming):
        return from_behind(final + through * incoming, "ctx", 1)

    carry_in = lax.fori_loop(0, lax.axis_size("ctx") - 1, relay_turn, jnp.zeros_like(final))
    state = local_state + cumulative * carry_in[:, None, :]
    gated = (state.reshape(count, -1) * branch).astype(jnp.bfloat16)
    partial_out = jnp.dot(gated, w_out, preferred_element_type=jnp.float32)
    share = lax.psum_scatter(
        partial_out.reshape(batch, rows_dev, width), "mp", scatter_dimension=2, tiled=True
    )
    resid_share = (tokens.astype(jnp.float32) + share).astype(jnp.bfloat16)
    wide_share = resid_share.astype(jnp.float32)
    squares = lax.psum(jnp.sum(wide_share * wide_share, axis=-1), "mp")
    normed_share = (wide_share * lax.rsqrt(squares[..., None] / width + EPSILON)).astype(
        jnp.bfloat16
    )
    normed_two = lax.all_gather(normed_share, "mp", axis=2, tiled=True).reshape(count, width)
    base = lax.axis_index("ctx") * rows_dev
    positions = base + jnp.arange(rows_dev, dtype=jnp.int32)
    query = jnp.dot(normed_two, w_query, preferred_element_type=jnp.float32).reshape(
        batch, rows_dev, -1, HD
    )
    query = (rotate(query, positions) * HD ** (-0.5)).astype(jnp.bfloat16)
    key_local = jnp.dot(normed_two, w_key, preferred_element_type=jnp.float32).astype(jnp.bfloat16)
    value_local = jnp.dot(normed_two, w_value, preferred_element_type=jnp.float32).astype(
        jnp.bfloat16
    )
    key_raw, value_whole = (
        lax.all_gather(key_local, "mp", axis=1, tiled=True),
        lax.all_gather(value_local, "mp", axis=1, tiled=True),
    )
    keys = (
        rotate(key_raw.astype(jnp.float32).reshape(batch, rows_dev, 1, HD), positions)
        .astype(jnp.bfloat16)
        .reshape(batch, rows_dev, HD)
    )
    paired = jnp.stack([keys, value_whole.reshape(batch, rows_dev, HD)])
    earlier = [from_behind(paired, "ctx", distance) for distance in (4, 3, 2, 1)]
    window_kv = jnp.concatenate(earlier + [paired], axis=2)
    span = window_kv.shape[2]
    scores = jnp.einsum("bshc,bkc->bhsk", query, window_kv[0], preferred_element_type=jnp.float32)
    rows = jnp.arange(rows_dev, dtype=jnp.int32)[:, None]
    cols = jnp.arange(span, dtype=jnp.int32)[None, :]
    distance_back = rows + WINDOW - cols
    valid = (distance_back >= 0) & (distance_back < WINDOW) & (cols >= WINDOW - base)
    masked = jnp.where(valid, scores, -1e30)
    top = jnp.max(masked, axis=-1, keepdims=True)
    weights = jnp.where(valid, jnp.exp(masked - top), 0.0)
    probs = (weights / jnp.sum(weights, axis=-1, keepdims=True)).astype(jnp.bfloat16)
    attended = (
        jnp.einsum("bhsk,bkc->bshc", probs, window_kv[1], preferred_element_type=jnp.float32)
        .astype(jnp.bfloat16)
        .reshape(count, -1)
    )
    partial_attn = jnp.dot(attended, w_attn_out, preferred_element_type=jnp.float32)
    share_attn = lax.psum_scatter(
        partial_attn.reshape(batch, rows_dev, width).astype(jnp.bfloat16),
        "mp",
        scatter_dimension=2,
        tiled=True,
    ).astype(jnp.float32)
    return (resid_share.astype(jnp.float32) + share_attn).astype(jnp.bfloat16)


def solution(mesh):
    in_specs = (
        P(None, "ctx", "mp"),
        P(None, "mp"),
        P(None, "mp"),
        P(None, "mp"),
        P("mp", None, None),
        P("mp", None, None),
        P("mp"),
        P("mp", None),
        P(None, "mp"),
        P(None, "mp"),
        P(None, "mp"),
        P("mp", None),
    )
    out_specs = P(None, "ctx", "mp")
    return jax.shard_map(
        on_device, mesh=mesh, in_specs=in_specs, out_specs=out_specs, check_vma=False
    )
```

profile of v0, /device:TPU:13, one launch (start us, length us, event | category | flops | bytes accessed | tf_op | source)
XLA Modules:
  0.0 692.8 jit_solution(18178669790131596333)
XLA Ops:
  8.2 80.0 %all-gather.3.cloned.1.call-done = bf16[1,512,4096]{2,1,0:T(8,128)(2,1)} async-done(((bf16[1,512,1024]{2,1,0:T(8,128)(2,1)}), bf16[1,512,4096]{2,1,0:T(8,128)(2,1)}) %all-gather.3.cloned.1.call-update) | async-done | bytes 4194320 | tf_op jit(solution)/shard_map/all_gather | solution.py:61
  88.2 3.2 fusion.1
  91.6 4.6 fusion.23
  96.2 3.9 collective-permute-start.1
  213.7 2.8 pad.127
  219.2 2.7 pad.126
  221.9 2.8 pad.145
  224.7 2.7 pad.144
  228.8 39.5 %while.10 = (s32[]{:T(128)}, f32[1,512]{1,0:T(1,128)S(1)}, f32[1,512]{1,0:T(1,128)S(1)}, f32[1,512]{1,0:T(1,128)S(1)}, s32[]{:T(128)}) while((s32[]{:T(128)}, f32[1,512]{1,0:T(1,128)S(1)}, f32[1,512]{1,0:T(1,128)S(1)}, f32[1,512]{1,0:T(1,128)S(1)}, s32[]{:T(128)}) %tuple.51), condition=%wide.region_2.3_spmd, body=%wide.region_1.2_spmd.sunk | while | flops 1026 | bytes 16485 | solution.py:95
  228.9 4.2 collective-permute-start
  233.8 4.2 collective-permute-start
  239.3 3.5 collective-permute-start
  245.1 2.6 collective-permute-start
  247.8 3.2 collective-permute-done
  252.8 3.9 collective-permute-done
  258.6 3.9 collective-permute-done
  264.4 3.9 collective-permute-done
  268.3 13.8 %convolution_bitcast_fusion = f32[1,512,4096]{2,1,0:T(8,128)} fusion(bf16[512,4096]{1,0:T(8,128)(2,1)} %param.21, bf16[4096,512]{1,0:T(8,128)(2,1)} %param.15, bf16[1,512,4096]{2,1,0:T(8,128)(2,1)} %all-gather.3.cloned.1.call-done, f32[512]{0:T(512)S(1)} %copy-done.22, f32[1,512,512]{2,1,0:T(8,128)} %pad.144, f32[1,512,512]{2,1,0:T(8,128)} %pad.145, ...), kind=kOutput, calls=%fused_computation.10 | convolution fusion | flops 4304928768 | bytes 25169920 | tf_op jit(solution)/shard_map/dot_general | solution.py:98
  282.2 146.8 %reduce-scatter.3.cloned.1.call-done = f32[1,512,1024]{2,1,0:T(8,128)} async-done(((f32[1,512,4096]{2,1,0:T(8,128)}), f32[1,512,1024]{2,1,0:T(8,128)}) %reduce-scatter.3.cloned.1.call-update) | async-done | bytes 2097168 | tf_op jit(solution)/shard_map/reduce_scatter | solution.py:99
  431.0 7.9 %psum.7 = f32[1,512]{1,0:T(1,128)S(1)} all-reduce(f32[1,512]{1,0:T(1,128)S(1)} %bitcast.148), channel_id=1, replica_groups=mesh['ctx'=8,'mp'=4] {'mp'}, use_global_device_ids=true, to_apply=%region_5.6 | all-reduce | flops 512 | bytes 4096 | tf_op jit(solution)/shard_map/psum | solution.py:104
  440.2 6.7 copy.31
  450.0 70.4 %all-gather.5.cloned.1.call-done = bf16[1,512,4096]{2,1,0:T(8,128)(2,1)} async-done(((bf16[1,512,1024]{2,1,0:T(8,128)(2,1)}), bf16[1,512,4096]{2,1,0:T(8,128)(2,1)}) %all-gather.5.cloned.1.call-update) | async-done | bytes 4194320 | tf_op jit(solution)/shard_map/all_gather | solution.py:108
  520.4 3.7 fusion.38
  524.2 12.3 %all_gather.14 = bf16[512,256]{0,1:T(8,128)(2,1)S(1)} all-gather(bf16[512,64]{0,1:T(8,128)(2,1)S(1)} %fusion.38), channel_id=1, replica_groups=mesh['ctx'=8,'mp'=4] {'mp'}, dimensions={1}, use_global_device_ids=true | all-gather | bytes 327680 | tf_op jit(solution)/shard_map/all_gather | solution.py:120
  538.6 11.2 %all_gather.15 = bf16[512,256]{0,1:T(8,128)(2,1)S(1)} all-gather(bf16[512,64]{0,1:T(8,128)(2,1)S(1)} %fusion.41), channel_id=1, replica_groups=mesh['ctx'=8,'mp'=4] {'mp'}, dimensions={1}, use_global_device_ids=true | all-gather | bytes 327680 | tf_op jit(solution)/shard_map/all_gather | solution.py:121
  552.4 3.1 collective-permute-start.4
  555.5 6.7 collective-permute-start.5
  564.8 7.6 %collective-permute-done.3 = bf16[2,1,512,256]{2,3,1,0:T(8,128)(2,1)S(1)} collective-permute-done((bf16[2,1,512,256]{2,3,1,0:T(8,128)(2,1)S(1)}, bf16[2,1,512,256]{2,3,1,0:T(8,128)(2,1)S(1)}, u32[]{:S(2)}, u32[]{:S(2)}) %collective-permute-start.3) | collective-permute-done | bytes 524320 | tf_op jit(solution)/shard_map/ppermute | solution.py:16
  572.4 2.8 collective-permute-done.4
  579.7 3.9 fusion.35
  583.6 4.4 fusion.4
  588.1 95.7 %reduce-scatter.5.cloned.1.call-done = bf16[1,512,1024]{2,1,0:T(8,128)(2,1)} async-done(((bf16[1,512,4096]{2,1,0:T(8,128)(2,1)}), bf16[1,512,1024]{2,1,0:T(8,128)(2,1)}) %reduce-scatter.5.cloned.1.call-update) | async-done | bytes 1048592 | tf_op jit(solution)/shard_map/reduce_scatter | solution.py:147
  (250 shorter events, 150.0 us)
Async XLA Ops:
  6.5 513.9 %copy-start = (bf16[4096,64]{0,1:T(8,128)(2,1)S(1)}, bf16[4096,64]{0,1:T(8,128)(2,1)}, u32[]{:S(2)}) copy-start(bf16[4096,64]{0,1:T(8,128)(2,1)} %param.23) | copy-start | bytes 1572868
  6.5 81.6 %all-gather.3.cloned.1.call-start = ((), (), s32[]{:S(2)}) async-start(), calls=%async_computation.2 | async-start | bytes 5242880 | tf_op jit(solution)/shard_map/all_gather | solution.py:61
  7.3 421.7 %reduce-scatter.3.cloned.1.call-start = ((), (), s32[]{:S(2)}) async-start(), calls=%async_computation.3 | async-start | bytes 10485760 | tf_op jit(solution)/shard_map/reduce_scatter | solution.py:99
  91.6 4.6 copy-start.21
  91.6 8.6 %copy-start.20 = (f32[512]{0:T(512)S(1)}, f32[512]{0:T(512)}, u32[]{:S(2)}) copy-start(f32[512]{0:T(512)} %param.20) | copy-start | bytes 6148
  96.2 6.3 copy-start.23
  96.2 4.7 collective-permute-start.1
  195.5 16.6 %copy-start.12 = (f32[1,63,512]{2,1,0:T(8,128)S(1)}, f32[1,63,512]{2,1,0:T(8,128)}, u32[]{:S(2)}) copy-start(f32[1,63,512]{2,1,0:T(8,128)} %slice.385) | copy-start | bytes 387076
  200.3 11.9 %copy-start.19 = (f32[1,1,512]{2,1,0:T(1,128)S(1)}, f32[1,1,512]{2,1,0:T(1,128)}, u32[]{:S(2)}) copy-start(f32[1,1,512]{2,1,0:T(1,128)} %slice.453) | copy-start | bytes 6148
  207.4 5.8 copy-start.9
  216.7 7.9 %copy-start.15 = (f32[1,1,512]{2,1,0:T(1,128)S(1)}, f32[1,1,512]{2,1,0:T(1,128)}, u32[]{:S(2)}) copy-start(f32[1,1,512]{2,1,0:T(1,128)} %slice.451) | copy-start | bytes 6148
  219.1 5.5 copy-start.7
  219.1 8.3 %copy-start.8 = (f32[1,512,512]{2,1,0:T(8,128)S(1)}, f32[1,512,512]{2,1,0:T(8,128)}, u32[]{:S(2)}) copy-start(f32[1,512,512]{2,1,0:T(8,128)} %pad.127) | copy-start | bytes 3145732
  219.1 49.2 %copy-start.22 = (f32[512]{0:T(512)S(1)}, f32[512]{0:T(512)}, u32[]{:S(2)}) copy-start(f32[512]{0:T(512)} %copy-done.21) | copy-start | bytes 6148
  228.9 4.9 collective-permute-start
  233.8 5.5 collective-permute-start
  239.3 5.8 collective-permute-start
  245.1 5.8 collective-permute-start
  250.9 5.8 collective-permute-start
  256.7 5.8 collective-permute-start
  262.5 5.8 collective-permute-start
  282.1 146.9 %copy-start.6 = (bf16[1,512,1024]{2,1,0:T(8,128)(2,1)S(1)}, bf16[1,512,1024]{2,1,0:T(8,128)(2,1)}, u32[]{:S(2)}) copy-start(bf16[1,512,1024]{2,1,0:T(8,128)(2,1)} %param.14) | copy-start | bytes 3145732
  282.1 238.3 %all-gather.5.cloned.1.call-start = ((), (), s32[]{:S(2)}) async-start(), calls=%async_computation.4 | async-start | bytes 5242880 | tf_op jit(solution)/shard_map/all_gather | solution.py:108
  440.2 243.5 %reduce-scatter.5.cloned.1.call-start = ((), (), s32[]{:S(2)}) async-start(), calls=%async_computation.5 | async-start | bytes 5242880 | tf_op jit(solution)/shard_map/reduce_scatter | solution.py:147
  446.9 90.3 %copy-start.10 = (bf16[4096,64]{0,1:T(8,128)(2,1)S(1)}, bf16[4096,64]{0,1:T(8,128)(2,1)}, u32[]{:S(2)}) copy-start(bf16[4096,64]{0,1:T(8,128)(2,1)} %param.24) | copy-start | bytes 1572868
  520.4 16.7 %copy-start.2 = (bf16[1,512,4096]{2,1,0:T(8,128)(2,1)S(1)}, bf16[1,512,4096]{2,1,0:T(8,128)(2,1)}, u32[]{:S(2)}) copy-start(bf16[1,512,4096]{2,1,0:T(8,128)(2,1)} %all-gather.5.cloned.1.call-done) | copy-start | bytes 12582916
  524.2 38.0 %copy-start.5 = (bf16[512,4096]{1,0:T(8,128)(2,1)S(1)}, bf16[512,4096]{1,0:T(8,128)(2,1)}, u32[]{:S(2)}) copy-start(bf16[512,4096]{1,0:T(8,128)(2,1)} %copy.31) | copy-start | bytes 12582916
  549.8 14.9 %collective-permute-start.2 = (bf16[2,1,512,256]{2,3,1,0:T(8,128)(2,1)S(1)}, bf16[2,1,512,256]{2,3,1,0:T(8,128)(2,1)S(1)}, u32[]{:S(2)}, u32[]{:S(2)}) collective-permute-start(bf16[2,1,512,256]{2,3,1,0:T(8,128)(2,1)S(1)} %pad_maximum_fusion.3), channel_id=1, source_target_pairs={{0,16},{4,20},{8,24},{12,28},{1,17},{5,21},{9,25},{13,29},{2,18},{... | collective-permute-start | bytes 1572872 | tf_op jit(solution)/shard_map/ppermute | solution.py:16
  551.1 21.3 %collective-permute-start.3 = (bf16[2,1,512,256]{2,3,1,0:T(8,128)(2,1)S(1)}, bf16[2,1,512,256]{2,3,1,0:T(8,128)(2,1)S(1)}, u32[]{:S(2)}, u32[]{:S(2)}) collective-permute-start(bf16[2,1,512,256]{2,3,1,0:T(8,128)(2,1)S(1)} %pad_maximum_fusion.3), channel_id=1, source_target_pairs={{0,12},{4,16},{8,20},{12,24},{16,28},{1,13},{5,17},{9,21},{13,25},... | collective-permute-start | bytes 1572872 | tf_op jit(solution)/shard_map/ppermute | solution.py:16
  552.4 22.8 %collective-permute-start.4 = (bf16[2,1,512,256]{2,3,1,0:T(8,128)(2,1)S(1)}, bf16[2,1,512,256]{2,3,1,0:T(8,128)(2,1)S(1)}, u32[]{:S(2)}, u32[]{:S(2)}) collective-permute-start(bf16[2,1,512,256]{2,3,1,0:T(8,128)(2,1)S(1)} %pad_maximum_fusion.3), channel_id=1, source_target_pairs={{0,8},{4,12},{8,16},{12,20},{16,24},{20,28},{1,9},{5,13},{9,17},{1... | collective-permute-start | bytes 1572872 | tf_op jit(solution)/shard_map/ppermute | solution.py:16
  555.5 19.7 %collective-permute-start.5 = (bf16[2,1,512,256]{2,3,1,0:T(8,128)(2,1)S(1)}, bf16[2,1,512,256]{2,3,1,0:T(8,128)(2,1)S(1)}, u32[]{:S(2)}, u32[]{:S(2)}) collective-permute-start(bf16[2,1,512,256]{2,3,1,0:T(8,128)(2,1)S(1)} %pad_maximum_fusion.3), channel_id=1, source_target_pairs={{0,4},{4,8},{8,12},{12,16},{16,20},{20,24},{24,28},{1,5},{5,9},{9,... | collective-permute-start | bytes 1572872 | tf_op jit(solution)/shard_map/ppermute | solution.py:16
  583.6 102.7 %copy-start.1 = (bf16[4096,64]{0,1:T(8,128)(2,1)S(1)}, bf16[4096,64]{0,1:T(8,128)(2,1)}, u32[]{:S(2)}) copy-start(bf16[4096,64]{0,1:T(8,128)(2,1)} %param.23) | copy-start | bytes 1572868
  (9 other events, 24.2 us)
Sparse Core Ops, SparseCore 0:
  8.9 79.2 all-gather.2
  282.2 146.7 reduce-scatter.2
  440.3 80.0 all-gather.4
  588.2 95.4 reduce-scatter.4
where the time goes:
time: 698 us; the launch traced here: 693 us
  waiting for transfers between devices  424 us (61%)
  local copies, waits for them, and re-layouts  101 us (14%)
  other arithmetic  48.7 us (7%)
  matrix products  37 us (5%)
  starting transfers between devices  36.7 us (5%)
  blocking collectives  31.4 us (4%)
  between operations  13.9 us (2%)
    reduce_scatter x1, waiting for transfers between devices, on_device(): lax.psum_scatter(partial_out.reshape(batch, rows_dev, width), 'mp', scatt...  147 us
    reduce_scatter x1, waiting for transfers between devices, on_device(): lax.psum_scatter(partial_attn.reshape(batch, rows_dev, width).astype(jnp....  95.7 us
    all_gather x1, waiting for transfers between devices, on_device(): full = lax.all_gather(tokens, 'mp', axis=2, tiled=True)  80 us
    slice x60, local copies, waits for them, and re-layouts, on_device(): lax.associative_scan(combine_steps, (decay, scaled), axis=1)  77.3 us
    all_gather x1, waiting for transfers between devices, on_device(): lax.all_gather(normed_share, 'mp', axis=2, tiled=True).reshape(count, width)  70.4 us
    ppermute x12, starting transfers between devices, from_behind(): return lax.ppermute(x, axis, pairs)  36.5 us
    ppermute x12, waiting for transfers between devices, from_behind(): return lax.ppermute(x, axis, pairs)  30.2 us
    add x16, other arithmetic, combine_steps(): return (earlier[0] * later[0], later[0] * earlier[1] + later[1])  18.5 us
  transfers between devices with their start and end apart: 16, of which 14 were waited for; matrix products, arithmetic and copies ran while one was open for 2% of the time, Pallas kernels for 0%

commit v1 on v0

--- a/solution.py
+++ b/solution.py
@@ -1,6 +1,10 @@
+import functools
+
 import jax
 import jax.numpy as jnp
 from jax import lax
+from jax.experimental import pallas as pl
+from jax.experimental.pallas import tpu as pltpu
 from jax.sharding import PartitionSpec as P
 
 HD = 256
@@ -37,8 +41,85 @@
     )
 
 
-def combine_steps(earlier, later):
-    return (earlier[0] * later[0], later[0] * earlier[1] + later[1])
+def recurrence_kernel(
+    count, decay_ref, scaled_ref, branch_ref, out_ref, local, cumulative, edge, got, send, recv
+):
+    me = lax.axis_index("ctx")
+    barrier = pltpu.get_barrier_semaphore()
+    for step in range(1, count):
+        pl.semaphore_signal(barrier, inc=1, device_id={"ctx": lax.rem(me + step, count)})
+    rows, width = decay_ref.shape
+    tile = 8
+    place = lax.broadcasted_iota(jnp.int32, (tile, width), 0)
+
+    def advance(index, carried):
+        state, product = carried
+        at = pl.ds(pl.multiple_of(index * tile, tile), tile)
+        a = decay_ref[at, :]
+        b = scaled_ref[at, :]
+        for shift in (1, 2, 4):
+            inside = place >= shift
+            a_back = jnp.where(inside, pltpu.roll(a, shift, 0), 1.0)
+            b_back = jnp.where(inside, pltpu.roll(b, shift, 0), 0.0)
+            b = a * b_back + b
+            a = a * a_back
+        b = b + a * state
+        a = a * product
+        local[at, :] = b
+        cumulative[at, :] = a
+        return b[tile - 1 :, :], a[tile - 1 :, :]
+
+    start = (jnp.zeros((1, width), jnp.float32), jnp.ones((1, width), jnp.float32))
+    state, product = lax.fori_loop(0, rows // tile, advance, start, unroll=4)
+    edge[0:1, :] = state
+    edge[1:2, :] = product
+    pl.semaphore_wait(barrier, count - 1)
+    copies = []
+    for step in range(1, count):
+        copy = pltpu.make_async_remote_copy(
+            src_ref=edge,
+            dst_ref=got.at[step],
+            send_sem=send.at[step],
+            recv_sem=recv.at[step],
+            device_id={"ctx": lax.rem(me + step, count)},
+        )
+        copy.start()
+        copies.append(copy)
+    for copy in copies:
+        copy.wait()
+    carry = jnp.zeros((1, width), jnp.float32)
+    for step in range(count - 1, 0, -1):
+        fresh = got[step, 0:1, :] + got[step, 1:2, :] * carry
+        carry = jnp.where(me >= step, fresh, 0.0)
+
+    def finish(index, _):
+        at = pl.ds(pl.multiple_of(index * 16, 16), 16)
+        whole = local[at, :] + cumulative[at, :] * carry
+        out_ref[at, :] = (whole * branch_ref[at, :]).astype(out_ref.dtype)
+        return 0
+
+    lax.fori_loop(0, rows // 16, finish, 0, unroll=4)
+
+
+def recurrence(decay, scaled, branch):
+    rows, width = decay.shape
+    count = lax.axis_size("ctx")
+    vmem = pl.BlockSpec(memory_space=pltpu.VMEM)
+    return pl.pallas_call(
+        functools.partial(recurrence_kernel, count),
+        out_shape=jax.ShapeDtypeStruct((rows, width), jnp.bfloat16),
+        in_specs=[vmem] * 3,
+        out_specs=vmem,
+        scratch_shapes=[
+            pltpu.VMEM((rows, width), jnp.float32),
+            pltpu.VMEM((rows, width), jnp.float32),
+            pltpu.VMEM((2, width), jnp.float32),
+            pltpu.VMEM((count, 2, width), jnp.float32),
+            pltpu.SemaphoreType.DMA((count,)),
+            pltpu.SemaphoreType.DMA((count,)),
+        ],
+        compiler_params=pltpu.CompilerParams(collective_id=0, has_side_effects=True),
+    )(decay, scaled, branch)
 
 
 def on_device(
@@ -85,41 +166,32 @@
     log_decay = -8.0 * rate_gate * jax.nn.softplus(-lam)
     decay = jnp.exp(log_decay)
     scaled = admit_gate * convolved * jnp.sqrt(-jnp.expm1(2.0 * log_decay))
-    cumulative, local_state = lax.associative_scan(combine_steps, (decay, scaled), axis=1)
-    through = cumulative[:, -1, :]
-    final = local_state[:, -1, :]
-
-    def relay_turn(step, incoming):
-        return from_behind(final + through * incoming, "ctx", 1)
-
-    carry_in = lax.fori_loop(0, lax.axis_size("ctx") - 1, relay_turn, jnp.zeros_like(final))
-    state = local_state + cumulative * carry_in[:, None, :]
-    gated = (state.reshape(count, -1) * branch).astype(jnp.bfloat16)
+    channels = decay.shape[-1]
+    gated = recurrence(
+        decay.reshape(count, channels), scaled.reshape(count, channels), branch
+    )
     partial_out = jnp.dot(gated, w_out, preferred_element_type=jnp.float32)
     share = lax.psum_scatter(
-        partial_out.reshape(batch, rows_dev, width), "mp", scatter_dimension=2, tiled=True
-    )
-    resid_share = (tokens.astype(jnp.float32) + share).astype(jnp.bfloat16)
-    wide_share = resid_share.astype(jnp.float32)
-    squares = lax.psum(jnp.sum(wide_share * wide_share, axis=-1), "mp")
-    normed_share = (wide_share * lax.rsqrt(squares[..., None] / width + EPSILON)).astype(
-        jnp.bfloat16
-    )
-    normed_two = lax.all_gather(normed_share, "mp", axis=2, tiled=True).reshape(count, width)
+        partial_out.astype(jnp.bfloat16).reshape(batch, rows_dev, width),
+        "mp",
+        scatter_dimension=2,
+        tiled=True,
+    )
+    resid_share = (tokens.astype(jnp.float32) + share.astype(jnp.float32)).astype(jnp.bfloat16)
+    resid = lax.all_gather(resid_share, "mp", axis=2, tiled=True)
+    normed_two = normalize(resid).astype(jnp.bfloat16).reshape(count, width)
     base = lax.axis_index("ctx") * rows_dev
     positions = base + jnp.arange(rows_dev, dtype=jnp.int32)
-    query = jnp.dot(normed_two, w_query, preferred_element_type=jnp.float32).reshape(
-        batch, rows_dev, -1, HD
-    )
-    query = (rotate(query, positions) * HD ** (-0.5)).astype(jnp.bfloat16)
     key_local = jnp.dot(normed_two, w_key, preferred_element_type=jnp.float32).astype(jnp.bfloat16)
     value_local = jnp.dot(normed_two, w_value, preferred_element_type=jnp.float32).astype(
         jnp.bfloat16
     )
-    key_raw, value_whole = (
-        lax.all_gather(key_local, "mp", axis=1, tiled=True),
-        lax.all_gather(value_local, "mp", axis=1, tiled=True),
-    )
+    both = lax.all_gather(jnp.stack([key_local, value_local]), "mp", axis=2, tiled=True)
+    key_raw, value_whole = both[0], both[1]
+    query = jnp.dot(normed_two, w_query, preferred_element_type=jnp.float32).reshape(
+        batch, rows_dev, -1, HD
+    )
+    query = (rotate(query, positions) * HD ** (-0.5)).astype(jnp.bfloat16)
     keys = (
         rotate(key_raw.astype(jnp.float32).reshape(batch, rows_dev, 1, HD), positions)
         .astype(jnp.bfloat16)

time: 698 us -> 459 us (0.66)
  local copies, waits for them, and re-layouts: 101 us -> 13.9 us
  waiting for transfers between devices: 424 us -> 338 us
  other arithmetic: 48.7 us -> 22.8 us
  starting transfers between devices: 36.7 us -> 14 us
  blocking collectives: 31.4 us -> 13.8 us
  Pallas kernels: 0 us -> 7.32 us
    slice x60 -> x0, local copies, waits for them, and re-layouts: 77.3 us -> none  [on_device(): lax.associative_scan(combine_steps, (decay, scaled), axis=1)]
    reduce_scatter x1, waiting for transfers between devices: 147 us -> 76.7 us  [on_device(): lax.psum_scatter(partial_out.astype(jnp.bfloat16).reshape(batch, rows_dev...]
    ppermute x12 -> x5, starting transfers between devices: 36.5 us -> 13.7 us  [from_behind(): return lax.ppermute(x, axis, pairs)]
    add x38 -> x0, other arithmetic: 19.5 us -> none  [the longest x16 18.5 us: combine_steps(): return (earlier[0] * later[0], later[0] * earlier[1] + later[1])]
    reduce_scatter x1, waiting for transfers between devices: 95.7 us -> 77 us  [on_device(): lax.psum_scatter(partial_attn.reshape(batch, rows_dev, width).astype(jnp....]
    pad x32 -> x0, local copies, waits for them, and re-layouts: 13 us -> none  [on_device(): lax.associative_scan(combine_steps, (decay, scaled), axis=1)]
    all_gather x2 -> x1, blocking collectives: 23.5 us -> 13.8 us  [on_device(): lax.all_gather(jnp.stack([key_local, value_local]), 'mp', axis=2, tiled=T...]
    psum x1 -> x0, blocking collectives: 7.94 us -> none  [on_device(): squares = lax.psum(jnp.sum(wide_share * wide_share, axis=-1), 'mp')]
  transfers between devices with their start and end apart: 16 -> 9, of which waited for: 14 -> 5; matrix products, arithmetic and copies ran while one was open for 2% -> 4% of each run, Pallas kernels for 0% -> 0%
where the time goes in v1:
time: 459 us; the launch traced here: 457 us
  waiting for transfers between devices  338 us (74%)
  matrix products  33.6 us (7%)
  other arithmetic  22.8 us (5%)
  starting transfers between devices  14 us (3%)
  local copies, waits for them, and re-layouts  13.9 us (3%)
  blocking collectives  13.8 us (3%)
  between operations  13.5 us (3%)
  Pallas kernels  7.32 us (2%)
    all_gather x1, waiting for transfers between devices, on_device(): full = lax.all_gather(tokens, 'mp', axis=2, tiled=True)  79.3 us
    reduce_scatter x1, waiting for transfers between devices, on_device(): lax.psum_scatter(partial_attn.reshape(batch, rows_dev, width).astype(jnp....  77 us
    reduce_scatter x1, waiting for transfers between devices, on_device(): lax.psum_scatter(partial_out.astype(jnp.bfloat16).reshape(batch, rows_dev...  76.7 us
    all_gather x1, waiting for transfers between devices, on_device(): resid = lax.all_gather(resid_share, 'mp', axis=2, tiled=True)  69.6 us
    ppermute x5, waiting for transfers between devices, from_behind(): return lax.ppermute(x, axis, pairs)  34.3 us
    all_gather x1, blocking collectives, on_device(): lax.all_gather(jnp.stack([key_local, value_local]), 'mp', axis=2, tiled=T...  13.8 us
    ppermute x5, starting transfers between devices, from_behind(): return lax.ppermute(x, axis, pairs)  13.7 us
  transfers between devices with their start and end apart: 9, of which 5 were waited for; matrix products, arithmetic and copies ran while one was open for 4% of the time, Pallas kernels for 0%

profile of v1, /device:TPU:13, one launch (start us, length us, event | category | flops | bytes accessed | tf_op | source)
XLA Modules:
  0.0 456.5 jit_solution(2336392984760156729)
XLA Ops:
  8.9 79.3 %all-gather.3.cloned.1.call-done = bf16[1,512,4096]{2,1,0:T(8,128)(2,1)} async-done(((bf16[1,512,1024]{2,1,0:T(8,128)(2,1)}), bf16[1,512,4096]{2,1,0:T(8,128)(2,1)}) %all-gather.3.cloned.1.call-update) | async-done | bytes 4194320 | tf_op jit(solution)/shard_map/all_gather | solution.py:142
  88.2 3.2 fusion.1
  91.6 4.7 %fusion.23 = f32[512,512]{1,0:T(8,128)S(1)} fusion(bf16[4096,512]{1,0:T(8,128)(2,1)} %param.14, bf16[1,512,4096]{2,1,0:T(8,128)(2,1)S(1)} %copy-done.7, f32[512]{0:T(512)S(1)} %add_rsqrt_fusion.1), kind=kOutput, calls=%fused_computation.34 | convolution fusion | flops 2153775104 | bytes 9439232 | tf_op jit(solution)/shard_map/dot_general | solution.py:145
  96.3 3.8 collective-permute-start
  100.2 3.5 fusion.63.branch_ref
  105.2 2.6 fusion.30
  107.8 2.6 copy.30
  110.3 1.3 copy.31
  111.6 1.6 copy.29
  114.3 3.2 multiply_bitcast_fusion.scaled_ref
  117.5 7.3 %shard_map.118 = bf16[512,512]{1,0:T(8,128)(2,1)} custom-call(f32[512,512]{1,0:T(8,128)} %multiply_exponential_fusion.decay_ref, f32[512,512]{1,0:T(8,128)} %multiply_bitcast_fusion.scaled_ref, f32[512,512]{1,0:T(8,128)} %fusion.63.branch_ref), custom_call_target="tpu_custom_call" | custom-call | tf_op jit(solution)/shard_map/pallas_call | solution.py:108
  124.8 6.7 %fusion.6 = bf16[1,512,4096]{2,1,0:T(8,128)(2,1)} fusion(bf16[512,512]{1,0:T(8,128)(2,1)} %shard_map.118, bf16[512,4096]{1,0:T(8,128)(2,1)} %param.19), kind=kOutput, calls=%fused_computation.15 | convolution fusion | flops 2149580800 | bytes 8912896 | tf_op jit(solution)/shard_map/dot_general | solution.py:173
  131.6 76.7 %reduce-scatter.3.cloned.1.call-done = bf16[1,512,1024]{2,1,0:T(8,128)(2,1)} async-done(((bf16[1,512,4096]{2,1,0:T(8,128)(2,1)}), bf16[1,512,1024]{2,1,0:T(8,128)(2,1)}) %reduce-scatter.3.cloned.1.call-update) | async-done | bytes 1048592 | tf_op jit(solution)/shard_map/reduce_scatter | solution.py:174
  208.3 2.6 add_convert_fusion.1
  211.1 6.5 %copy.33 = bf16[512,4096]{1,0:T(8,128)(2,1)} copy(bf16[512,4096]{0,1:T(8,128)(2,1)} %bitcast.134) | data formatting | bytes 8388608 | tf_op jit(solution)/shard_map/dot_general | solution.py:191
  218.2 1.9 fusion.13
  220.1 69.6 %all-gather.5.cloned.1.call-done = bf16[1,512,4096]{2,1,0:T(8,128)(2,1)} async-done(((bf16[1,512,1024]{2,1,0:T(8,128)(2,1)}), bf16[1,512,4096]{2,1,0:T(8,128)(2,1)}) %all-gather.5.cloned.1.call-update) | async-done | bytes 4194320 | tf_op jit(solution)/shard_map/all_gather | solution.py:181
  289.7 3.2 fusion.3
  293.2 1.4 fusion.44
  294.6 1.5 fusion.47
  296.1 13.8 %all_gather.11 = bf16[2,512,256]{1,2,0:T(8,128)(2,1)S(1)} all-gather(bf16[2,512,64]{1,2,0:T(8,128)(2,1)S(1)} %pad_maximum_fusion.2), channel_id=1, replica_groups=mesh['ctx'=8,'mp'=4] {'mp'}, dimensions={2}, use_global_device_ids=true | all-gather | bytes 655360 | tf_op jit(solution)/shard_map/all_gather | solution.py:189
  310.7 5.3 %collective-permute-start.4 = (bf16[2,1,512,256]{2,3,1,0:T(8,128)(2,1)S(1)}, bf16[2,1,512,256]{2,3,1,0:T(8,128)(2,1)S(1)}, u32[]{:S(2)}, u32[]{:S(2)}) collective-permute-start(bf16[2,1,512,256]{2,3,1,0:T(8,128)(2,1)S(1)} %pad_maximum_fusion.1), channel_id=1, source_target_pairs={{0,4},{4,8},{8,12},{12,16},{16,20},{20,24},{24,28},{1,5},{5,9},{9,... | collective-permute-start | bytes 1572872 | tf_op jit(solution)/shard_map/ppermute | solution.py:20
  316.0 1.9 collective-permute-start.3
  317.9 1.3 collective-permute-start.2
  320.5 2.4 fusion.25
  323.1 34.3 %collective-permute-done.1 = bf16[2,1,512,256]{2,3,1,0:T(8,128)(2,1)S(1)} collective-permute-done((bf16[2,1,512,256]{2,3,1,0:T(8,128)(2,1)S(1)}, bf16[2,1,512,256]{2,3,1,0:T(8,128)(2,1)S(1)}, u32[]{:S(2)}, u32[]{:S(2)}) %collective-permute-start.1) | collective-permute-done | bytes 524320 | tf_op jit(solution)/shard_map/ppermute | solution.py:20
  357.7 2.0 fusion
  359.6 2.4 fusion.5
  362.1 3.9 fusion.35
  366.0 4.4 fusion.7
  370.4 77.0 %reduce-scatter.5.cloned.1.call-done = bf16[1,512,1024]{2,1,0:T(8,128)(2,1)} async-done(((bf16[1,512,4096]{2,1,0:T(8,128)(2,1)}), bf16[1,512,1024]{2,1,0:T(8,128)(2,1)}) %reduce-scatter.5.cloned.1.call-update) | async-done | bytes 1048592 | tf_op jit(solution)/shard_map/reduce_scatter | solution.py:219
  447.4 2.6 add_convert_fusion
  (63 shorter events, 8.5 us)
Async XLA Ops:
  6.5 286.4 %copy-start = (bf16[4096,64]{0,1:T(8,128)(2,1)S(1)}, bf16[4096,64]{0,1:T(8,128)(2,1)}, u32[]{:S(2)}) copy-start(bf16[4096,64]{0,1:T(8,128)(2,1)} %param.22) | copy-start | bytes 1572868
  6.5 81.6 %all-gather.3.cloned.1.call-start = ((), (), s32[]{:S(2)}) async-start(), calls=%async_computation.2 | async-start | bytes 5242880 | tf_op jit(solution)/shard_map/all_gather | solution.py:142
  7.3 201.0 %reduce-scatter.3.cloned.1.call-start = ((), (), s32[]{:S(2)}) async-start(), calls=%async_computation.3 | async-start | bytes 5242880 | tf_op jit(solution)/shard_map/reduce_scatter | solution.py:174
  88.2 3.4 copy-start.7
  91.6 8.5 %copy-start.9 = (bf16[4096,512]{1,0:T(8,128)(2,1)S(1)}, bf16[4096,512]{1,0:T(8,128)(2,1)}, u32[]{:S(2)}) copy-start(bf16[4096,512]{1,0:T(8,128)(2,1)} %param.13) | copy-start | bytes 12582916
  96.3 7.4 %collective-permute-start = (f32[1,3,512]{2,1,0:T(4,128)S(1)}, f32[1,3,512]{2,1,0:T(4,128)S(1)}, u32[]{:S(2)}, u32[]{:S(2)}) collective-permute-start(f32[1,3,512]{2,1,0:T(4,128)S(1)} %slice.73), channel_id=1, source_target_pairs={{0,4},{4,8},{8,12},{12,16},{16,20},{20,24},{24,28},{1,5},{5,9},{9,... | collective-permute-start | bytes 18440 | tf_op jit(solution)/shard_map/ppermute | solution.py:20
  103.7 0.9 copy-start.11
  105.1 6.5 %copy-start.8 = (f32[2,512,256]{1,2,0:T(8,128)}, f32[2,512,256]{1,2,0:T(8,128)S(1)}, u32[]{:S(2)}) copy-start(f32[2,512,256]{1,2,0:T(8,128)S(1)} %fusion.33) | copy-start | bytes 3145732
  131.5 76.8 %copy-start.3 = (bf16[1,512,1024]{2,1,0:T(8,128)(2,1)S(1)}, bf16[1,512,1024]{2,1,0:T(8,128)(2,1)}, u32[]{:S(2)}) copy-start(bf16[1,512,1024]{2,1,0:T(8,128)(2,1)} %param.12) | copy-start | bytes 3145732
  131.5 158.2 %all-gather.5.cloned.1.call-start = ((), (), s32[]{:S(2)}) async-start(), calls=%async_computation.4 | async-start | bytes 5242880 | tf_op jit(solution)/shard_map/all_gather | solution.py:181
  210.9 236.5 %reduce-scatter.5.cloned.1.call-start = ((), (), s32[]{:S(2)}) async-start(), calls=%async_computation.5 | async-start | bytes 5242880 | tf_op jit(solution)/shard_map/reduce_scatter | solution.py:219
  289.7 3.4 copy-start.5
  293.2 1.5 copy-start.10
  296.1 24.4 %copy-start.6 = (bf16[512,4096]{1,0:T(8,128)(2,1)S(1)}, bf16[512,4096]{1,0:T(8,128)(2,1)}, u32[]{:S(2)}) copy-start(bf16[512,4096]{1,0:T(8,128)(2,1)} %copy.33) | copy-start | bytes 12582916
  310.7 46.9 %collective-permute-start.4 = (bf16[2,1,512,256]{2,3,1,0:T(8,128)(2,1)S(1)}, bf16[2,1,512,256]{2,3,1,0:T(8,128)(2,1)S(1)}, u32[]{:S(2)}, u32[]{:S(2)}) collective-permute-start(bf16[2,1,512,256]{2,3,1,0:T(8,128)(2,1)S(1)} %pad_maximum_fusion.1), channel_id=1, source_target_pairs={{0,4},{4,8},{8,12},{12,16},{16,20},{20,24},{24,28},{1,5},{5,9},{9,... | collective-permute-start | bytes 1572872 | tf_op jit(solution)/shard_map/ppermute | solution.py:20
  316.0 41.5 %collective-permute-start.3 = (bf16[2,1,512,256]{2,3,1,0:T(8,128)(2,1)S(1)}, bf16[2,1,512,256]{2,3,1,0:T(8,128)(2,1)S(1)}, u32[]{:S(2)}, u32[]{:S(2)}) collective-permute-start(bf16[2,1,512,256]{2,3,1,0:T(8,128)(2,1)S(1)} %pad_maximum_fusion.1), channel_id=1, source_target_pairs={{0,8},{4,12},{8,16},{12,20},{16,24},{20,28},{1,9},{5,13},{9,17},{1... | collective-permute-start | bytes 1572872 | tf_op jit(solution)/shard_map/ppermute | solution.py:20
  317.9 39.5 %collective-permute-start.2 = (bf16[2,1,512,256]{2,3,1,0:T(8,128)(2,1)S(1)}, bf16[2,1,512,256]{2,3,1,0:T(8,128)(2,1)S(1)}, u32[]{:S(2)}, u32[]{:S(2)}) collective-permute-start(bf16[2,1,512,256]{2,3,1,0:T(8,128)(2,1)S(1)} %pad_maximum_fusion.1), channel_id=1, source_target_pairs={{0,12},{4,16},{8,20},{12,24},{16,28},{1,13},{5,17},{9,21},{13,25},... | collective-permute-start | bytes 1572872 | tf_op jit(solution)/shard_map/ppermute | solution.py:20
  319.2 38.2 %collective-permute-start.1 = (bf16[2,1,512,256]{2,3,1,0:T(8,128)(2,1)S(1)}, bf16[2,1,512,256]{2,3,1,0:T(8,128)(2,1)S(1)}, u32[]{:S(2)}, u32[]{:S(2)}) collective-permute-start(bf16[2,1,512,256]{2,3,1,0:T(8,128)(2,1)S(1)} %pad_maximum_fusion.1), channel_id=1, source_target_pairs={{0,16},{4,20},{8,24},{12,28},{1,17},{5,21},{9,25},{13,29},{2,18},{... | collective-permute-start | bytes 1572872 | tf_op jit(solution)/shard_map/ppermute | solution.py:20
  362.0 3.9 copy-start.4
  366.0 84.0 %copy-start.1 = (bf16[4096,64]{0,1:T(8,128)(2,1)S(1)}, bf16[4096,64]{0,1:T(8,128)(2,1)}, u32[]{:S(2)}) copy-start(bf16[4096,64]{0,1:T(8,128)(2,1)} %param.22) | copy-start | bytes 1572868
  370.4 77.0 %copy-start.2 = (bf16[1,512,1024]{2,1,0:T(8,128)(2,1)S(1)}, bf16[1,512,1024]{2,1,0:T(8,128)(2,1)}, u32[]{:S(2)}) copy-start(bf16[1,512,1024]{2,1,0:T(8,128)(2,1)} %add_convert_fusion.1) | copy-start | bytes 3145732
Sparse Core Ops, SparseCore 0:
  8.9 79.2 all-gather.2
  131.7 76.5 reduce-scatter.2
  211.0 78.6 all-gather.4
  370.5 76.8 reduce-scatter.4

commit v2 on v1

--- a/solution.py
+++ b/solution.py
@@ -122,6 +122,316 @@
     )(decay, scaled, branch)
 
 
+CHUNKS = 4
+
+
+def greet(me, count):
+    barrier = pltpu.get_barrier_semaphore()
+    for step in range(1, count):
+        pl.semaphore_signal(barrier, inc=1, device_id={"mp": lax.rem(me + step, count)})
+    pl.semaphore_wait(barrier, count - 1)
+
+
+def each(chunks, body):
+    def turn(chunk, _):
+        body(chunk)
+        return 0
+
+    lax.fori_loop(0, chunks, turn, 0)
+
+
+def span_of(chunk, rows):
+    return pl.ds(pl.multiple_of(chunk * rows, rows), rows)
+
+
+class Line:
+    def __init__(self, me, count):
+        self.me, self.count = me, count
+
+    def steps(self, way):
+        return self.me + 1 if way == 0 else self.me - 1
+
+    def has_next(self, way):
+        return self.me < self.count - 1 if way == 0 else self.me > 0
+
+    def has_last(self, way):
+        return self.me > 0 if way == 0 else self.me < self.count - 1
+
+    def copy(self, way, src, dst, send, recv):
+        return pltpu.make_async_remote_copy(
+            src_ref=src,
+            dst_ref=dst,
+            send_sem=send,
+            recv_sem=recv,
+            device_id={"mp": self.steps(way)},
+        )
+
+
+def gather_part(line, own, out_ref, send, recv, cols, rows, chunks):
+    me, count = line.me, line.count
+
+    def region(owner, chunk):
+        return out_ref.at[
+            span_of(chunk, rows), pl.ds(pl.multiple_of(owner * cols, cols), cols)
+        ]
+
+    def source(way, step):
+        return me - step if way == 0 else me + step
+
+    def moved(way, step, chunk):
+        owner = source(way, step)
+        place = region(owner, chunk)
+        return line.copy(
+            way,
+            own.at[span_of(chunk, rows), :] if step == 0 else place,
+            place,
+            send.at[way, step, chunk],
+            recv.at[way, step, chunk],
+        )
+
+    def there(way, step):
+        return source(way, step) >= 0 if way == 0 else source(way, step) < count
+
+    def begin(chunk):
+        for way in (0, 1):
+
+            @pl.when(line.has_next(way))
+            def _():
+                moved(way, 0, chunk).start()
+
+    def relay():
+        for step in range(1, count):
+
+            def turn(chunk, step=step):
+                for way in (0, 1):
+
+                    @pl.when(there(way, step))
+                    def _():
+                        place = region(source(way, step), chunk)
+                        line.copy(
+                            1 - way,
+                            place,
+                            place,
+                            send.at[way, step - 1, chunk],
+                            recv.at[way, step - 1, chunk],
+                        ).wait_recv()
+
+                    @pl.when(jnp.logical_and(there(way, step), line.has_next(way)))
+                    def _():
+                        moved(way, step, chunk).start()
+
+            each(chunks, turn)
+
+        for step in range(count):
+
+            def turn(chunk, step=step):
+                for way in (0, 1):
+
+                    @pl.when(jnp.logical_and(there(way, step), line.has_next(way)))
+                    def _():
+                        moved(way, step, chunk).wait_send()
+
+            each(chunks, turn)
+
+    return region, begin, relay
+
+
+def reduce_part(line, part_ref, base_ref, held, send, recv, cols, rows, chunks):
+    me, count = line.me, line.count
+
+    def goal(way, step):
+        return count - 1 - step if way == 0 else step
+
+    def beyond(way, step):
+        return goal(way, step) > me if way == 0 else goal(way, step) < me
+
+    def moved(way, step, chunk):
+        place = held.at[way, step, span_of(chunk, rows), :]
+        return line.copy(
+            way,
+            held.at[way, step, span_of(chunk, rows), :],
+            place,
+            send.at[way, step, chunk],
+            recv.at[way, step, chunk],
+        )
+
+    def arrived(way, step, chunk):
+        place = held.at[way, step, span_of(chunk, rows), :]
+        line.copy(
+            1 - way, place, place, send.at[way, step, chunk], recv.at[way, step, chunk]
+        ).wait_recv()
+
+    def term(owner, chunk):
+        return part_ref[
+            span_of(chunk, rows), pl.ds(pl.multiple_of(owner * cols, cols), cols)
+        ]
+
+    def outward():
+        for step in range(count - 1):
+
+            def turn(chunk, step=step):
+                for way in (0, 1):
+                    at = span_of(chunk, rows)
+
+                    @pl.when(jnp.logical_and(beyond(way, step), line.has_last(way)))
+                    def _():
+                        arrived(way, step, chunk)
+                        total = held[way, step, at, :].astype(jnp.float32) + term(
+                            goal(way, step), chunk
+                        ).astype(jnp.float32)
+                        held[way, step, at, :] = total.astype(held.dtype)
+
+                    @pl.when(
+                        jnp.logical_and(
+                            beyond(way, step), jnp.logical_not(line.has_last(way))
+                        )
+                    )
+                    def _():
+                        held[way, step, at, :] = term(goal(way, step), chunk)
+
+                    @pl.when(beyond(way, step))
+                    def _():
+                        moved(way, step, chunk).start()
+
+            each(chunks, turn)
+
+    def finish(chunk, total):
+        at = span_of(chunk, rows)
+        total[...] = term(me, chunk).astype(jnp.float32)
+        for way in (0, 1):
+            for step in range(count):
+
+                @pl.when(jnp.logical_and(goal(way, step) == me, line.has_last(way)))
+                def _():
+                    arrived(way, step, chunk)
+                    total[...] += held[way, step, at, :].astype(jnp.float32)
+
+        return (base_ref[at, :].astype(jnp.float32) + total[...]).astype(jnp.bfloat16)
+
+    def settle():
+        for step in range(count - 1):
+
+            def turn(chunk, step=step):
+                for way in (0, 1):
+
+                    @pl.when(beyond(way, step))
+                    def _():
+                        moved(way, step, chunk).wait_send()
+
+            each(chunks, turn)
+
+    return outward, finish, settle
+
+
+def gather_kernel(count, chunks, own_ref, out_ref, send, recv, local):
+    me = lax.axis_index("mp")
+    rows, cols = own_ref.shape[0] // chunks, own_ref.shape[1]
+    greet(me, count)
+    line = Line(me, count)
+    region, begin, relay = gather_part(line, own_ref, out_ref, send, recv, cols, rows, chunks)
+
+    def turn(chunk):
+        begin(chunk)
+
+    each(chunks, turn)
+    mine = out_ref.at[:, pl.ds(pl.multiple_of(me * cols, cols), cols)]
+    kept = pltpu.make_async_copy(own_ref, mine, local.at[0])
+    kept.start()
+    relay()
+    kept.wait()
+
+
+def reduce_gather_kernel(
+    count, chunks, part_ref, base_ref, own_ref, out_ref, held, total, sends, recvs, send, recv, local
+):
+    me = lax.axis_index("mp")
+    rows, cols = base_ref.shape[0] // chunks, base_ref.shape[1]
+    greet(me, count)
+    line = Line(me, count)
+    outward, finish, settle = reduce_part(
+        line, part_ref, base_ref, held, sends, recvs, cols, rows, chunks
+    )
+    region, begin, relay = gather_part(line, own_ref, out_ref, send, recv, cols, rows, chunks)
+    outward()
+
+    def turn(chunk):
+        own_ref[span_of(chunk, rows), :] = finish(chunk, total)
+        begin(chunk)
+
+    each(chunks, turn)
+    mine = out_ref.at[:, pl.ds(pl.multiple_of(me * cols, cols), cols)]
+    kept = pltpu.make_async_copy(own_ref, mine, local.at[0])
+    kept.start()
+    relay()
+    settle()
+    kept.wait()
+
+
+def reduce_kernel(count, chunks, part_ref, base_ref, own_ref, held, total, sends, recvs):
+    me = lax.axis_index("mp")
+    rows, cols = base_ref.shape[0] // chunks, base_ref.shape[1]
+    greet(me, count)
+    line = Line(me, count)
+    outward, finish, settle = reduce_part(
+        line, part_ref, base_ref, held, sends, recvs, cols, rows, chunks
+    )
+    outward()
+
+    def turn(chunk):
+        own_ref[span_of(chunk, rows), :] = finish(chunk, total)
+
+    each(chunks, turn)
+    settle()
+
+
+def gather(own, mark, chunks=CHUNKS):
+    count = lax.axis_size("mp")
+    rows, cols = own.shape
+    return pl.pallas_call(
+        functools.partial(gather_kernel, count, chunks),
+        out_shape=jax.ShapeDtypeStruct((rows, cols * count), own.dtype),
+        in_specs=[pl.BlockSpec(memory_space=pltpu.VMEM)],
+        out_specs=pl.BlockSpec(memory_space=pl.ANY),
+        scratch_shapes=[
+            pltpu.SemaphoreType.DMA((2, count, chunks)),
+            pltpu.SemaphoreType.DMA((2, count, chunks)),
+            pltpu.SemaphoreType.DMA((1,)),
+        ],
+        compiler_params=pltpu.CompilerParams(collective_id=mark, has_side_effects=True),
+    )(own)
+
+
+def reduce_scatter(part, base, mark, spread, chunks=CHUNKS):
+    count = lax.axis_size("mp")
+    rows, cols = base.shape
+    vmem = pl.BlockSpec(memory_space=pltpu.VMEM)
+    own = jax.ShapeDtypeStruct((rows, cols), base.dtype)
+    semaphores = pltpu.SemaphoreType.DMA((2, count, chunks))
+    scratch = [
+        pltpu.VMEM((2, count, rows, cols), base.dtype),
+        pltpu.VMEM((rows // chunks, cols), jnp.float32),
+        semaphores,
+        semaphores,
+    ]
+    if spread:
+        return pl.pallas_call(
+            functools.partial(reduce_gather_kernel, count, chunks),
+            out_shape=(own, jax.ShapeDtypeStruct((rows, cols * count), base.dtype)),
+            in_specs=[vmem, vmem],
+            out_specs=(vmem, pl.BlockSpec(memory_space=pl.ANY)),
+            scratch_shapes=scratch + [semaphores, semaphores, pltpu.SemaphoreType.DMA((1,))],
+            compiler_params=pltpu.CompilerParams(collective_id=mark, has_side_effects=True),
+        )(part, base)
+    return pl.pallas_call(
+        functools.partial(reduce_kernel, count, chunks),
+        out_shape=own,
+        in_specs=[vmem, vmem],
+        out_specs=vmem,
+        scratch_shapes=scratch,
+        compiler_params=pltpu.CompilerParams(collective_id=mark, has_side_effects=True),
+    )(part, base)
+
+
 def on_device(
     tokens,
     w_branch,
@@ -139,7 +449,8 @@
     batch, rows_dev, cols_dev = tokens.shape
     count = batch * rows_dev
     width = w_branch.shape[0]
-    full = lax.all_gather(tokens, "mp", axis=2, tiled=True)
+    tokens_flat = tokens.reshape(count, cols_dev)
+    full = gather(tokens_flat, 1)
     normed = normalize(full).astype(jnp.bfloat16).reshape(count, width)
     branch = jax.nn.gelu(jnp.dot(normed, w_branch, preferred_element_type=jnp.float32))
     inner = jnp.dot(normed, w_input, preferred_element_type=jnp.float32).reshape(
@@ -156,13 +467,21 @@
         )
     blocks = w_rate.shape[0]
     block_width = w_rate.shape[1]
-    grouped = convolved.astype(jnp.bfloat16).reshape(batch, rows_dev, blocks, block_width)
-    rate_gate = jax.nn.sigmoid(
-        jnp.einsum("bsnc,ncd->bsnd", grouped, w_rate, preferred_element_type=jnp.float32)
-    ).reshape(batch, rows_dev, -1)
-    admit_gate = jax.nn.sigmoid(
-        jnp.einsum("bsnc,ncd->bsnd", grouped, w_admit, preferred_element_type=jnp.float32)
-    ).reshape(batch, rows_dev, -1)
+    low = convolved.astype(jnp.bfloat16).reshape(count, -1)
+
+    def gate(weights):
+        products = [
+            jnp.dot(
+                low[:, block * block_width : (block + 1) * block_width],
+                weights[block],
+                preferred_element_type=jnp.float32,
+            )
+            for block in range(blocks)
+        ]
+        return jax.nn.sigmoid(jnp.concatenate(products, axis=-1)).reshape(batch, rows_dev, -1)
+
+    rate_gate = gate(w_rate)
+    admit_gate = gate(w_admit)
     log_decay = -8.0 * rate_gate * jax.nn.softplus(-lam)
     decay = jnp.exp(log_decay)
     scaled = admit_gate * convolved * jnp.sqrt(-jnp.expm1(2.0 * log_decay))
@@ -171,14 +490,9 @@
         decay.reshape(count, channels), scaled.reshape(count, channels), branch
     )
     partial_out = jnp.dot(gated, w_out, preferred_element_type=jnp.float32)
-    share = lax.psum_scatter(
-        partial_out.astype(jnp.bfloat16).reshape(batch, rows_dev, width),
-        "mp",
-        scatter_dimension=2,
-        tiled=True,
-    )
-    resid_share = (tokens.astype(jnp.float32) + share.astype(jnp.float32)).astype(jnp.bfloat16)
-    resid = lax.all_gather(resid_share, "mp", axis=2, tiled=True)
+    resid_share, resid = reduce_scatter(
+        partial_out.astype(jnp.bfloat16), tokens_flat, 2, spread=True
+    )
     normed_two = normalize(resid).astype(jnp.bfloat16).reshape(count, width)
     base = lax.axis_index("ctx") * rows_dev
     positions = base + jnp.arange(rows_dev, dtype=jnp.int32)
@@ -216,13 +530,8 @@
         .reshape(count, -1)
     )
     partial_attn = jnp.dot(attended, w_attn_out, preferred_element_type=jnp.float32)
-    share_attn = lax.psum_scatter(
-        partial_attn.reshape(batch, rows_dev, width).astype(jnp.bfloat16),
-        "mp",
-        scatter_dimension=2,
-        tiled=True,
-    ).astype(jnp.float32)
-    return (resid_share.astype(jnp.float32) + share_attn).astype(jnp.bfloat16)
+    result = reduce_scatter(partial_attn.astype(jnp.bfloat16), resid_share, 3, spread=False)
+    return result.reshape(batch, rows_dev, cols_dev)
 
 
 def solution(mesh):

time: 459 us -> 410 us (0.89)
  waiting for transfers between devices: 338 us -> 30.6 us
  Pallas kernels: 7.32 us -> 281 us
  between operations: 13.5 us -> 0.45 us
  starting transfers between devices: 14 us -> 21.9 us
  other arithmetic: 22.8 us -> 17.6 us
    pallas_call x0 -> x3, Pallas kernels: none -> 274 us  [the longest x1 127 us: reduce_scatter(): pl.pallas_call(functools.partial(reduce_gather_kernel, count, chunks), ou...]
    reduce_scatter x2 -> x0, waiting for transfers between devices: 154 us -> none  [the longest x1 77 us: on_device(): lax.psum_scatter(partial_attn.reshape(batch, rows_dev, width).astype(jnp....]
    all_gather x2 -> x0, waiting for transfers between devices: 149 us -> none  [the longest x1 79.3 us: on_device(): full = lax.all_gather(tokens, 'mp', axis=2, tiled=True)]
    unnamed x28 -> x32, local copies, waits for them, and re-layouts: 0.94 us -> 9.35 us
    ppermute x5, starting transfers between devices: 13.7 us -> 21.9 us  [from_behind(): return lax.ppermute(x, axis, pairs)]
    dot_general x1 -> x0, local copies, waits for them, and re-layouts: 6.5 us -> none  [on_device(): jnp.dot(normed_two, w_query, preferred_element_type=jnp.float32)]
    convert_element_type x3 -> x0, other arithmetic: 5.65 us -> none  [the longest x1 2.59 us: on_device(): return (resid_share.astype(jnp.float32) + share_attn).astype(jnp.bfloat16)]
    reshape x3 -> x0, local copies, waits for them, and re-layouts: 5.42 us -> none  [the longest x2 2.86 us: on_device(): rate_gate = jax.nn.sigmoid(jnp.einsum('bsnc,ncd->bsnd', grouped, w_rate,...]
  transfers between devices with their start and end apart: 9 -> 5, of which waited for: 5 -> 1; matrix products, arithmetic and copies ran while one was open for 4% -> 5% of each run, Pallas kernels for 0% -> 0%
where the time goes in v2:
time: 410 us; the launch traced here: 409 us
  Pallas kernels  281 us (69%)
  matrix products  35.3 us (9%)
  waiting for transfers between devices  30.6 us (7%)
  starting transfers between devices  21.9 us (5%)
  other arithmetic  17.6 us (4%)
  blocking collectives  12.2 us (3%)
  local copies, waits for them, and re-layouts  10.2 us (2%)
    pallas_call x1, Pallas kernels, reduce_scatter(): pl.pallas_call(functools.partial(reduce_gather_kernel, count, chunks), ou...  127 us
    pallas_call x1, Pallas kernels, reduce_scatter(): pl.pallas_call(functools.partial(reduce_kernel, count, chunks), out_shape...  76.4 us
    pallas_call x1, Pallas kernels, gather(): pl.pallas_call(functools.partial(gather_kernel, count, chunks), out_shape...  71.1 us
    ppermute x5, waiting for transfers between devices, from_behind(): return lax.ppermute(x, axis, pairs)  30.6 us
    ppermute x5, starting transfers between devices, from_behind(): return lax.ppermute(x, axis, pairs)  21.9 us
    all_gather x1, blocking collectives, on_device(): lax.all_gather(jnp.stack([key_local, value_local]), 'mp', axis=2, tiled=T...  12.2 us
    unnamed x32, local copies, waits for them, and re-layouts  9.35 us
  transfers between devices with their start and end apart: 5, of which 1 were waited for; matrix products, arithmetic and copies ran while one was open for 5% of the time, Pallas kernels for 0%

profile of v2, /device:TPU:13, one launch (start us, length us, event | category | flops | bytes accessed | tf_op | source)
XLA Modules:
  0.0 409.3 jit_solution(13376869915224887600)
XLA Ops:
  0.0 71.1 %shard_map.118 = bf16[512,4096]{1,0:T(8,128)(2,1)} custom-call(bf16[512,1024]{1,0:T(8,128)(2,1)} %bitcast.108), custom_call_target="tpu_custom_call" | custom-call | tf_op jit(solution)/shard_map/pallas_call | solution.py:390
  71.1 3.2 fusion.1
  74.5 4.6 %fusion.14 = f32[512,512]{1,0:T(8,128)S(1)} fusion(bf16[4096,512]{1,0:T(8,128)(2,1)} %param.14, bf16[512,4096]{1,0:T(8,128)(2,1)S(1)} %copy-done.2, f32[512]{0:T(512)S(1)} %add_rsqrt_fusion.1), kind=kOutput, calls=%fused_computation.23 | convolution fusion | flops 2153775104 | bytes 9439232 | tf_op jit(solution)/shard_map/dot_general | solution.py:456
  79.1 4.5 %collective-permute-start = (f32[1,3,512]{2,1,0:T(4,128)S(1)}, f32[1,3,512]{2,1,0:T(4,128)S(1)}, u32[]{:S(2)}, u32[]{:S(2)}) collective-permute-start(f32[1,3,512]{2,1,0:T(4,128)S(1)} %slice.99), channel_id=1, source_target_pairs={{0,4},{4,8},{8,12},{12,16},{16,20},{20,24},{24,28},{1,5},{5,9},{9,... | collective-permute-start | bytes 18440 | tf_op jit(solution)/shard_map/ppermute | solution.py:20
  83.8 7.0 %fusion.35.branch_ref = f32[512,512]{1,0:T(8,128)} fusion(bf16[4096,512]{1,0:T(8,128)(2,1)} %param.13, bf16[512,4096]{1,0:T(8,128)(2,1)} %shard_map.118, f32[512]{0:T(512)S(1)} %add_rsqrt_fusion.1), kind=kOutput, calls=%fused_computation.50 | convolution fusion | flops 2155872256 | bytes 9439232 | tf_op jit(solution)/shard_map/dot_general | solution.py:455
  91.7 2.1 fusion.11
  95.3 1.4 fusion.43.decay_ref
  96.7 2.0 fusion.49.scaled_ref
  98.7 7.4 %shard_map.119 = bf16[512,512]{1,0:T(8,128)(2,1)} custom-call(f32[512,512]{1,0:T(8,128)} %fusion.43.decay_ref, f32[512,512]{1,0:T(8,128)} %fusion.49.scaled_ref, f32[512,512]{1,0:T(8,128)} %fusion.35.branch_ref), custom_call_target="tpu_custom_call" | custom-call | tf_op jit(solution)/shard_map/pallas_call | solution.py:108
  106.1 6.7 %convolution_convert_fusion.1.part_ref = bf16[512,4096]{1,0:T(8,128)(2,1)} fusion(bf16[512,512]{1,0:T(8,128)(2,1)} %shard_map.119, bf16[512,4096]{1,0:T(8,128)(2,1)} %param.19), kind=kOutput, calls=%fused_computation.14 | convolution fusion | flops 2149580800 | bytes 8912896 | tf_op jit(solution)/shard_map/dot_general | solution.py:492
  112.7 126.5 %shard_map.120 = (bf16[512,1024]{1,0:T(8,128)(2,1)}, bf16[512,4096]{1,0:T(8,128)(2,1)}) custom-call(bf16[512,4096]{1,0:T(8,128)(2,1)} %convolution_convert_fusion.1.part_ref, bf16[512,1024]{1,0:T(8,128)(2,1)} %bitcast.109), custom_call_target="tpu_custom_call" | custom-call | tf_op jit(solution)/shard_map/pallas_call | solution.py:417
  239.3 3.2 fusion.3
  242.7 1.5 fusion.21
  244.2 1.5 fusion.20
  245.7 12.2 %all_gather.3 = bf16[2,512,256]{1,2,0:T(8,128)(2,1)S(1)} all-gather(bf16[2,512,64]{1,2,0:T(8,128)(2,1)S(1)} %pad_maximum_fusion.2), channel_id=1, replica_groups=mesh['ctx'=8,'mp'=4] {'mp'}, dimensions={2}, use_global_device_ids=true | all-gather | bytes 655360 | tf_op jit(solution)/shard_map/all_gather | solution.py:503
  259.4 1.3 collective-permute-start.2
  260.7 1.3 collective-permute-start.1
  262.0 2.5 fusion.91
  265.3 12.6 %collective-permute-start.4 = (bf16[2,1,512,256]{2,3,1,0:T(8,128)(2,1)}, bf16[2,1,512,256]{2,3,1,0:T(8,128)(2,1)}, u32[]{:S(2)}, u32[]{:S(2)}) collective-permute-start(bf16[2,1,512,256]{2,3,1,0:T(8,128)(2,1)} %pad_maximum_fusion.1), channel_id=1, source_target_pairs={{0,4},{4,8},{8,12},{12,16},{16,20},{20,24},{24,28},{1,5},{5,9},{9,... | collective-permute-start | bytes 1572872 | tf_op jit(solution)/shard_map/ppermute | solution.py:20
  277.9 2.1 collective-permute-start.3
  281.3 1.1 copy.31
  282.6 30.5 %collective-permute-done.1 = bf16[2,1,512,256]{2,3,1,0:T(8,128)(2,1)} collective-permute-done((bf16[2,1,512,256]{2,3,1,0:T(8,128)(2,1)}, bf16[2,1,512,256]{2,3,1,0:T(8,128)(2,1)}, u32[]{:S(2)}, u32[]{:S(2)}) %collective-permute-start.1) | collective-permute-done | bytes 524320 | tf_op jit(solution)/shard_map/ppermute | solution.py:20
  313.1 1.1 constant_dynamic-update-slice_fusion.4
  314.2 1.1 constant_dynamic-update-slice_fusion.3
  315.3 1.1 constant_dynamic-update-slice_fusion.2
  316.4 1.1 constant_dynamic-update-slice_fusion.1
  317.5 2.4 fusion
  319.9 2.4 fusion.5
  322.4 3.9 fusion.17
  326.3 4.4 %convolution_convert_fusion.part_ref = bf16[512,4096]{1,0:T(8,128)(2,1)} fusion(bf16[512,512]{0,1:T(8,128)(2,1)S(1)} %bitcast.113, bf16[512,4096]{1,0:T(8,128)(2,1)S(1)} %copy-done.3), kind=kOutput, calls=%fused_computation.13 | convolution fusion | flops 2149580800 | bytes 8912896 | tf_op jit(solution)/shard_map/dot_general | solution.py:532
  330.7 76.4 %shard_map.121 = bf16[512,1024]{1,0:T(8,128)(2,1)} custom-call(bf16[512,4096]{1,0:T(8,128)(2,1)} %convolution_convert_fusion.part_ref, bf16[512,1024]{1,0:T(8,128)(2,1)} %get-tuple-element.8.base_ref), custom_call_target="tpu_custom_call" | custom-call | tf_op jit(solution)/shard_map/pallas_call | solution.py:425
  407.1 2.3 copy.39
  (54 shorter events, 6.5 us)
Async XLA Ops:
  0.0 242.5 %copy-start = (bf16[4096,64]{0,1:T(8,128)(2,1)S(1)}, bf16[4096,64]{0,1:T(8,128)(2,1)}, u32[]{:S(2)}) copy-start(bf16[4096,64]{0,1:T(8,128)(2,1)} %param.22) | copy-start | bytes 1572868
  71.1 3.5 copy-start.2
  74.5 9.2 %copy-start.8 = (f32[4,512]{1,0:T(4,128)S(1)}, f32[4,512]{1,0:T(4,128)}, u32[]{:S(2)}) copy-start(f32[4,512]{1,0:T(4,128)} %param.15) | copy-start | bytes 24580
  79.1 14.8 %collective-permute-start = (f32[1,3,512]{2,1,0:T(4,128)S(1)}, f32[1,3,512]{2,1,0:T(4,128)S(1)}, u32[]{:S(2)}, u32[]{:S(2)}) collective-permute-start(f32[1,3,512]{2,1,0:T(4,128)S(1)} %slice.99), channel_id=1, source_target_pairs={{0,4},{4,8},{8,12},{12,16},{16,20},{20,24},{24,28},{1,5},{5,9},{9,... | collective-permute-start | bytes 18440 | tf_op jit(solution)/shard_map/ppermute | solution.py:20
  83.7 10.1 %copy-start.9 = (f32[512]{0:T(512)S(1)}, f32[512]{0:T(512)}, u32[]{:S(2)}) copy-start(f32[512]{0:T(512)} %param.18) | copy-start | bytes 6148
  90.7 3.6 copy-start.6
  90.7 4.1 %copy-start.7 = (bf16[2,256,256]{2,1,0:T(8,128)(2,1)S(1)}, bf16[2,256,256]{2,1,0:T(8,128)(2,1)}, u32[]{:S(2)}) copy-start(bf16[2,256,256]{2,1,0:T(8,128)(2,1)} %param.17) | copy-start | bytes 786436
  239.3 3.5 copy-start.4
  242.7 1.5 copy-start.11
  245.7 16.3 %copy-start.10 = (bf16[4096,512]{1,0:T(8,128)(2,1)S(1)}, bf16[4096,512]{1,0:T(8,128)(2,1)}, u32[]{:S(2)}) copy-start(bf16[4096,512]{1,0:T(8,128)(2,1)} %param.20) | copy-start | bytes 12582916
  259.4 54.8 %collective-permute-start.2 = (bf16[2,1,512,256]{2,3,1,0:T(8,128)(2,1)}, bf16[2,1,512,256]{2,3,1,0:T(8,128)(2,1)}, u32[]{:S(2)}, u32[]{:S(2)}) collective-permute-start(bf16[2,1,512,256]{2,3,1,0:T(8,128)(2,1)} %pad_maximum_fusion.1), channel_id=1, source_target_pairs={{0,12},{4,16},{8,20},{12,24},{16,28},{1,13},{5,17},{9,21},{13,25},... | collective-permute-start | bytes 1572872 | tf_op jit(solution)/shard_map/ppermute | solution.py:20
  260.7 52.5 %collective-permute-start.1 = (bf16[2,1,512,256]{2,3,1,0:T(8,128)(2,1)}, bf16[2,1,512,256]{2,3,1,0:T(8,128)(2,1)}, u32[]{:S(2)}, u32[]{:S(2)}) collective-permute-start(bf16[2,1,512,256]{2,3,1,0:T(8,128)(2,1)} %pad_maximum_fusion.1), channel_id=1, source_target_pairs={{0,16},{4,20},{8,24},{12,28},{1,17},{5,21},{9,25},{13,29},{2,18},{... | collective-permute-start | bytes 1572872 | tf_op jit(solution)/shard_map/ppermute | solution.py:20
  265.3 51.1 %collective-permute-start.4 = (bf16[2,1,512,256]{2,3,1,0:T(8,128)(2,1)}, bf16[2,1,512,256]{2,3,1,0:T(8,128)(2,1)}, u32[]{:S(2)}, u32[]{:S(2)}) collective-permute-start(bf16[2,1,512,256]{2,3,1,0:T(8,128)(2,1)} %pad_maximum_fusion.1), channel_id=1, source_target_pairs={{0,4},{4,8},{8,12},{12,16},{16,20},{20,24},{24,28},{1,5},{5,9},{9,... | collective-permute-start | bytes 1572872 | tf_op jit(solution)/shard_map/ppermute | solution.py:20
  277.9 37.4 %collective-permute-start.3 = (bf16[2,1,512,256]{2,3,1,0:T(8,128)(2,1)}, bf16[2,1,512,256]{2,3,1,0:T(8,128)(2,1)}, u32[]{:S(2)}, u32[]{:S(2)}) collective-permute-start(bf16[2,1,512,256]{2,3,1,0:T(8,128)(2,1)} %pad_maximum_fusion.1), channel_id=1, source_target_pairs={{0,8},{4,12},{8,16},{12,20},{16,24},{20,28},{1,9},{5,13},{9,17},{1... | collective-permute-start | bytes 1572872 | tf_op jit(solution)/shard_map/ppermute | solution.py:20
  282.4 35.1 %copy-start.5 = (f32[1,512,2,128]{3,1,2,0:T(8,128)S(1)}, f32[1,512,2,128]{3,1,2,0:T(8,128)}, u32[]{:S(2)}) copy-start(f32[1,512,2,128]{3,1,2,0:T(8,128)} %copy.33) | copy-start | bytes 1572868
  322.4 3.9 copy-start.3
  330.7 78.7 %copy-start.1 = (bf16[4096,64]{0,1:T(8,128)(2,1)S(1)}, bf16[4096,64]{0,1:T(8,128)(2,1)}, u32[]{:S(2)}) copy-start(bf16[4096,64]{0,1:T(8,128)(2,1)} %param.22) | copy-start | bytes 1572868
